TPU v7x, 128 devices: a whole 4x4x4 slice. The times are simulated.
128 devices in a mesh: atom: 8 (over x, core), aux: 16 (over z, y).
Axes of the slice: x: 4, y: 4, z: 4, core: 2. Of those that a mesh axis runs over, the one named last changes fastest.
Arguments:
- three_index: bfloat16 [256, 16, 4, 128, 128], P('aux', 'atom'), may hold values from -0.09375 to 0.09375
- density: bfloat16 [2048, 2048], P(('atom', 'aux')), may hold values from -6 to 6
- pair_blocks: int32 [16, 4], replicated, may hold values from 0 to 15, as said below
- basis_counts: int32 [16], replicated, may hold values from 1 to 128, 1536 in all
Outputs:
- exchange_matrix: float32 [2048, 2048], P(('atom', 'aux'))
Inputs may be any that keep to these rules, and one draw needn't show every extreme that they name: `pair_blocks`: each row names 4 different basis blocks, the first being the row's own block.
All inputs are finite; a program needn't handle non-finite values.
Results may differ from a plain program's by a relative error of at most 0.0029.
Values may be sent and summed in bfloat16 or wider, within the bound.
No kernel may reach another device: no remote copies, remote signals or barrier semaphores. Data moves between devices by JAX's collectives and lax.ppermute only.
A program may use at most 192 MiB of HBM per device.

v0:
```python
import math
import jax
import jax.numpy as jnp
from jax import lax
from jax.sharding import PartitionSpec as P


def split_up(value, dim, size):
    lengths = value.shape
    parts = value.reshape(*lengths[:dim], size, lengths[dim] // size, *lengths[dim + 1 :])
    return jnp.moveaxis(parts, dim, 0)


def sent_and_summed(value, axis, dim):
    size = lax.axis_size(axis)
    parts = lax.all_to_all(split_up(value, dim, size), axis, 0, 0, tiled=True)
    return jnp.sum(parts, axis=0)


def per_device(three_index, density, pair_blocks, basis_counts):
    whole_density = lax.all_gather(density, ("atom", "aux"), axis=0, tiled=True)
    block_size = three_index.shape[-1]
    total_basis = whole_density.shape[1]
    total_blocks = total_basis // block_size
    own_blocks = three_index.shape[1]
    aux_here = three_index.shape[0]
    first_block = lax.axis_index("atom") * own_blocks
    live_slots = (jnp.arange(block_size)[None, :] < basis_counts[:, None]).astype(jnp.bfloat16)

    def masked(portion, offset):
        block_count = portion.shape[1]
        row_live = lax.dynamic_slice_in_dim(live_slots, offset, block_count, 0)
        partners = lax.dynamic_slice_in_dim(pair_blocks, offset, block_count, 0)
        col_live = live_slots[partners]
        cleaned = portion * row_live[None, :, None, :, None] * col_live[None, :, :, None, :]
        return (cleaned, partners)

    own_tensor, own_partners = masked(three_index, first_block)
    near_density = whole_density.reshape(total_blocks, block_size, total_basis)[own_partners]
    group_size = math.gcd(aux_here, 8)
    grouped = own_tensor.reshape((aux_here // group_size, group_size) + own_tensor.shape[1:])

    def contract(portion):
        product = jnp.einsum(
            "pmjab,mjbs->pmas", portion, near_density, preferred_element_type=jnp.float32
        )
        return product.astype(jnp.bfloat16)

    halfway = lax.map(contract, grouped).reshape(aux_here, own_blocks * block_size, total_basis)
    halfway_cols = halfway.reshape(aux_here, own_blocks * block_size, total_blocks, block_size)
    portion = lax.all_gather(three_index, "atom", axis=1, tiled=True)
    block_count = portion.shape[1]
    cleaned, partners = masked(portion, jnp.int32(0))
    contrib = jnp.einsum(
        "pmbc,pbjcn->mbjn", halfway_cols, cleaned, preferred_element_type=jnp.float32
    )
    placement = (partners.reshape(-1)[:, None] == jnp.arange(total_blocks)[None, :]).astype(
        jnp.float32
    )
    spread_out = jnp.einsum(
        "mqn,qk->mkn",
        contrib.reshape(contrib.shape[0], -1, block_size),
        placement,
        precision=lax.Precision.HIGHEST,
    )
    row_sums = spread_out.reshape(contrib.shape[0], total_basis)
    return sent_and_summed(row_sums, "aux", 0)


def solution(mesh):
    in_specs = (P("aux", "atom", None, None, None), P(("atom", "aux"), None), P(), P())
    out_specs = P(("atom", "aux"), None)
    return jax.shard_map(
        per_device, mesh=mesh, in_specs=in_specs, out_specs=out_specs, check_vma=False
    )
```

profile of v0, /device:TPU:0, one launch (start us, length us, event | category | flops | bytes accessed | tf_op | source)
XLA Modules:
  0.0 328.8 jit_solution(8203879094852832548)
XLA Ops:
  6.5 0.0 all-gather.5.cloned.1.call-start
  6.5 0.7 all-gather.5.cloned.1.call-update
  7.3 0.0 all-gather.3.cloned.1.call-start
  7.3 0.7 all-gather.3.cloned.1.call-update
  8.0 0.8 copy.10
  8.8 0.8 compare_select_fusion
  9.5 0.1 copy.12
  9.6 0.1 reshape.48
  9.7 0.7 compare_select_fusion.1
  10.4 0.1 copy.11
  10.5 0.1 reshape.40
  10.6 0.7 fusion.7
  11.3 0.6 gather_fusion.1
  11.9 0.6 gather_fusion
  12.5 0.1 eq.15
  12.6 4.5 %multiply_multiply_fusion.1 = bf16[16,2,4,128,128]{4,3,2,1,0:T(8,128)(2,1)} fusion(bf16[16,2,4,128,128]{4,3,2,1,0:T(8,128)(2,1)} %param.6, bf16[2,4,128]{2,1,0:T(4,128)(2,1)S(1)} %bitcast.57, bf16[2,128]{1,0:T(2,128)(2,1)S(1)} %constant_dynamic-slice_fusion.1), kind=kLoop, calls=%fused_computation.14 | loop fusion | flops 4194304 | bytes 8391168 | tf_op jit(solution)/shard_map/mul | solution.py:35
  17.2 66.0 %all-gather.5.cloned.1.call-done = bf16[2048,2048]{1,0:T(8,128)(2,1)} async-done(((bf16[16,2048]{1,0:T(8,128)(2,1)}), bf16[2048,2048]{1,0:T(8,128)(2,1)}) %all-gather.5.cloned.1.call-update) | async-done | bytes 8388624 | tf_op jit(solution)/shard_map/all_gather | solution.py:21
  83.2 6.1 %gather_fusion.2 = bf16[8,128,2048]{2,1,0:T(8,128)(2,1)} fusion(bf16[16,128,2048]{2,1,0:T(8,128)(2,1)} %bitcast.55, s32[1024]{0:T(1024)S(1)} %pad_clamp_fusion), kind=kCustom, calls=%fused_computation.2 | custom fusion | bytes 8388640 | tf_op jit(solution)/shard_map/gather | solution.py:39
  89.3 37.6 %while.10 = (s32[]{:T(128)}, bf16[2,8,2,128,2048]{4,3,2,1,0:T(8,128)(2,1)}, bf16[2,8,2,4,128,128]{5,4,3,2,1,0:T(8,128)(2,1)}, bf16[2,4,128,2048]{3,2,1,0:T(8,128)(2,1)}, s32[]{:T(128)}) while((s32[]{:T(128)}, bf16[2,8,2,128,2048]{4,3,2,1,0:T(8,128)(2,1)}, bf16[2,8,2,4,128,128]{5,4,3,2,1,0:T(8,128)(2,1)}, bf16[2,4,128,2048]{3,2,1,0:T(8,128)(2,1)}, ...), condition=%wide.region_1.2_spmd, body=%wide.region_0.1_spmd.sunk | while | flops 4299161600 | bytes 31458364 | solution.py:49
  89.3 9.7 %fusion.13 = bf16[1,8,2,128,2048]{4,3,1,2,0:T(8,128)(2,1)} fusion(bf16[2,4,128,2048]{3,2,1,0:T(8,128)(2,1)} %get-tuple-element.78, bf16[2,8,2,4,128,128]{5,4,3,2,1,0:T(8,128)(2,1)} %get-tuple-element.77, s32[]{:T(128)} %get-tuple-element.70), kind=kOutput, calls=%fused_computation.4.clone.1 | convolution fusion | flops 4299161600 | bytes 14680576 | tf_op jit(solution)/shard_map/while/body/eval_jaxpr/pmjab,mjbs->pmas/dot_general | solution.py:44
  99.0 10.4 %copy_dynamic-update-slice_fusion.2 = bf16[2,8,2,128,2048]{4,3,2,1,0:T(8,128)(2,1)} fusion(bf16[2,8,2,128,2048]{4,3,2,1,0:T(8,128)(2,1)} %get-tuple-element.71, s32[]{:T(128)} %get-tuple-element.70, bf16[1,8,2,128,2048]{4,3,1,2,0:T(8,128)(2,1)} %fusion.13), kind=kLoop, calls=%fused_computation.5.clone.1 | loop fusion | bytes 16777728 | tf_op jit(solution)/shard_map/while/body/jit(dynamic_update_index_in_dim)/dynamic_update_slice | solution.py:49
  109.4 9.2 %fusion.13 = bf16[1,8,2,128,2048]{4,3,1,2,0:T(8,128)(2,1)} fusion(bf16[2,4,128,2048]{3,2,1,0:T(8,128)(2,1)} %get-tuple-element.78, bf16[2,8,2,4,128,128]{5,4,3,2,1,0:T(8,128)(2,1)} %get-tuple-element.77, s32[]{:T(128)} %get-tuple-element.70), kind=kOutput, calls=%fused_computation.4.clone.1 | convolution fusion | flops 4299161600 | bytes 14680576 | tf_op jit(solution)/shard_map/while/body/eval_jaxpr/pmjab,mjbs->pmas/dot_general | solution.py:44
  118.7 8.2 %copy_dynamic-update-slice_fusion.2 = bf16[2,8,2,128,2048]{4,3,2,1,0:T(8,128)(2,1)} fusion(bf16[2,8,2,128,2048]{4,3,2,1,0:T(8,128)(2,1)} %get-tuple-element.71, s32[]{:T(128)} %get-tuple-element.70, bf16[1,8,2,128,2048]{4,3,1,2,0:T(8,128)(2,1)} %fusion.13), kind=kLoop, calls=%fused_computation.5.clone.1 | loop fusion | bytes 16777728 | tf_op jit(solution)/shard_map/while/body/jit(dynamic_update_index_in_dim)/dynamic_update_slice | solution.py:49
  126.9 9.9 %copy.29 = bf16[512,8,16,128]{3,2,1,0:T(8,128)(2,1)S(1)} copy(bf16[512,8,16,128]{3,1,2,0:T(8,128)(2,1)} %bitcast.52) | data formatting | bytes 33554432
  136.8 7.4 %bitcast_bitcast_fusion = bf16[16,256,16,128,1]{3,2,1,0,4:T(8,128)(2,1)} fusion(bf16[16,256,16,128]{3,2,1,0:T(8,128)(2,1)S(1)} %bitcast.50), kind=kLoop, calls=%fused_computation.12 | loop fusion | bytes 33554432 | tf_op jit(solution)/shard_map/reshape;reshape | solution.py:50
  144.3 94.0 %all-gather.3.cloned.1.call-done = bf16[16,16,4,128,128]{4,3,2,1,0:T(8,128)(2,1)} async-done(((bf16[16,2,4,128,128]{4,3,2,1,0:T(8,128)(2,1)}), bf16[16,16,4,128,128]{4,3,2,1,0:T(8,128)(2,1)}) %all-gather.3.cloned.1.call-update) | async-done | bytes 33554448 | tf_op jit(solution)/shard_map/all_gather | solution.py:51
  238.2 24.2 %fusion.2 = f32[16,4,128,256,1]{3,2,0,1,4:T(8,128)} fusion(bf16[16,256,16,128,1]{3,2,1,0,4:T(8,128)(2,1)} %bitcast_bitcast_fusion, bf16[16,16,4,128,128]{4,3,2,1,0:T(8,128)(2,1)} %all-gather.3.cloned.1.call-done, bf16[16,4,128]{2,1,0:T(4,128)(2,1)S(1)} %bitcast.56, bf16[16,128]{1,0:T(8,128)(2,1)S(1)} %fusion.7), kind=kOutput, calls=%fused_computation.9 | convolution fusion | flops 8623489024 | bytes 58740736 | tf_op jit(solution)/shard_map/pmbc,pbjcn->mbjn/dot_general | solution.py:54
  262.4 7.6 %copy.22 = f32[16,4,128,256,1]{3,2,1,0,4:T(8,128)} copy(f32[16,4,128,256,1]{3,2,0,1,4:T(8,128)} %fusion.2) | data formatting | bytes 16777216 | tf_op jit(solution)/shard_map/pmbc,pbjcn->mbjn/dot_general | solution.py:54
  270.0 8.7 %copy.17 = f32[256,64,128]{2,1,0:T(8,128)} copy(f32[256,64,128]{0,2,1:T(8,128)} %bitcast.51) | data formatting | bytes 16777216 | tf_op jit(solution)/shard_map/reshape | solution.py:62
  278.8 5.1 %convolution_bitcast_fusion = f32[256,16,128]{2,1,0:T(8,128)S(1)} fusion(f32[256,64,128]{2,1,0:T(8,128)} %copy.17, s32[64]{0:T(128)S(1)} %eq.15), kind=kOutput, calls=%fused_computation.15 | convolution fusion | flops 402654208 | bytes 10486016 | tf_op jit(solution)/shard_map/mqn,qk->mkn/dot_general | solution.py:60
  283.9 1.5 reshape_reshape.7
  285.4 35.8 %all_to_all.5 = f32[16,16,2048]{2,1,0:T(8,128)S(1)} all-to-all(f32[16,16,2048]{2,1,0:T(8,128)} %reshape_reshape.7), channel_id=1, replica_groups=mesh['atom'=8,'aux'=16] {'aux'}, dimensions={0} | all-to-all | bytes 4194304 | tf_op jit(solution)/shard_map/all_to_all | solution.py:16
  321.2 0.8 reduce_sum.9
  (4 shorter events, 0.0 us)
Async XLA Ops:
  6.5 76.6 %all-gather.5.cloned.1.call-start = ((), (), s32[]{:S(2)}) async-start(), calls=%async_computation.2 | async-start | bytes 8454144 | tf_op jit(solution)/shard_map/all_gather | solution.py:21
  7.3 231.0 %all-gather.3.cloned.1.call-start = ((), (), s32[]{:S(2)}) async-start(), calls=%async_computation.1 | async-start | bytes 37748736 | tf_op jit(solution)/shard_map/all_gather | solution.py:51
Sparse Core Ops, SparseCore 0:
  10.5 72.6 all-gather.4
  84.8 153.3 all-gather.2
where the time goes:
time: 329 us
  waiting for transfers between devices  161 us (49%)
  local copies, waits for them, and re-layouts  62.4 us (19%)
  matrix products  48.3 us (15%)
  blocking collectives  35.8 us (11%)
  between operations  13.5 us (4%)
  other arithmetic  7.45 us (2%)
    all_gather x1, waiting for transfers between devices, per_device(): portion = lax.all_gather(three_index, 'atom', axis=1, tiled=True)  94 us
    all_gather x1, waiting for transfers between devices, per_device(): whole_density = lax.all_gather(density, ('atom', 'aux'), axis=0, tiled=True)  66 us
    all_to_all x1, blocking collectives, sent_and_summed(): parts = lax.all_to_all(split_up(value, dim, size), axis, 0, 0, tiled=True)  35.8 us
    dot_general x1, matrix products, per_device(): jnp.einsum('pmbc,pbjcn->mbjn', halfway_cols, cleaned, preferred_element_t...  24.2 us
    dot_general x2, matrix products, contract(): jnp.einsum('pmjab,mjbs->pmas', portion, near_density, preferred_element_t...  18.9 us
    dynamic_update_slice x2, local copies, waits for them, and re-layouts, per_device(): lax.map(contract, grouped)  18.7 us
    unnamed x2, local copies, waits for them, and re-layouts  10.7 us
    reshape x1, local copies, waits for them, and re-layouts, per_device(): contrib.reshape(contrib.shape[0], -1, block_size)  8.72 us
  transfers between devices with their start and end apart: 2, of which 2 were waited for; matrix products, arithmetic and copies ran while one was open for 21% of the time, Pallas kernels for 0%

commit v1 on v0

--- a/solution.py
+++ b/solution.py
@@ -18,7 +18,12 @@
 
 
 def per_device(three_index, density, pair_blocks, basis_counts):
-    whole_density = lax.all_gather(density, ("atom", "aux"), axis=0, tiled=True)
+    whole_density = jnp.concatenate(
+        lax.all_to_all(
+            jnp.stack([density] * lax.axis_size(("atom", "aux"))), ("atom", "aux"), 0, 0
+        ),
+        axis=0,
+    )
     block_size = three_index.shape[-1]
     total_basis = whole_density.shape[1]
     total_blocks = total_basis // block_size

time: 329 us -> 353 us (1.073)
  waiting for transfers between devices: 161 us -> 175 us
  starting transfers between devices: 0.04 us -> 11.7 us
  blocking collectives: 35.8 us -> 31.3 us
    all_to_all x0 -> x1, waiting for transfers between devices: none -> 174 us  [per_device(): lax.all_to_all(jnp.stack([density] * lax.axis_size(('atom', 'aux'))), ('a...]
    all_gather x1, waiting for transfers between devices: 94 us -> 0.01 us  [per_device(): portion = lax.all_gather(three_index, 'atom', axis=1, tiled=True)]
    all_gather x1 -> x0, waiting for transfers between devices: 66 us -> none  [per_device(): whole_density = lax.all_gather(density, ('atom', 'aux'), axis=0, tiled=True)]
    all_to_all x0 -> x1, starting transfers between devices: none -> 11.7 us  [per_device(): lax.all_to_all(jnp.stack([density] * lax.axis_size(('atom', 'aux'))), ('a...]
    another operation x0 -> x1, local copies, waits for them, and re-layouts: none -> 5.1 us  [per_device(): jnp.stack([density] * lax.axis_size(('atom', 'aux')))]
    all_to_all x1, blocking collectives: 35.8 us -> 31.3 us  [sent_and_summed(): parts = lax.all_to_all(split_up(value, dim, size), axis, 0, 0, tiled=True)]
    unnamed x2 -> x6, local copies, waits for them, and re-layouts: 10.7 us -> 9.74 us
  transfers between devices with their start and end apart: 2 -> 2, of which waited for: 2 -> 1; matrix products, arithmetic and copies ran while one was open for 21% -> 20% of each run, Pallas kernels for 0% -> 0%
where the time goes in v1:
time: 353 us; the launch traced here: 351 us
  waiting for transfers between devices  175 us (50%)
  local copies, waits for them, and re-layouts  65.2 us (18%)
  matrix products  47.8 us (14%)
  blocking collectives  31.3 us (9%)
  between operations  13.5 us (4%)
  starting transfers between devices  11.7 us (3%)
  other arithmetic  6.16 us (2%)
    all_to_all x1, waiting for transfers between devices, per_device(): lax.all_to_all(jnp.stack([density] * lax.axis_size(('atom', 'aux'))), ('a...  174 us
    all_to_all x1, blocking collectives, sent_and_summed(): parts = lax.all_to_all(split_up(value, dim, size), axis, 0, 0, tiled=True)  31.3 us
    dot_general x1, matrix products, per_device(): jnp.einsum('pmbc,pbjcn->mbjn', halfway_cols, cleaned, preferred_element_t...  24.2 us
    dot_general x2, matrix products, contract(): jnp.einsum('pmjab,mjbs->pmas', portion, near_density, preferred_element_t...  18.5 us
    dynamic_update_slice x2, local copies, waits for them, and re-layouts, per_device(): lax.map(contract, grouped)  16.8 us
    all_to_all x1, starting transfers between devices, per_device(): lax.all_to_all(jnp.stack([density] * lax.axis_size(('atom', 'aux'))), ('a...  11.7 us
    unnamed x6, local copies, waits for them, and re-layouts  9.74 us
    reshape x1, local copies, waits for them, and re-layouts, per_device(): contrib.reshape(contrib.shape[0], -1, block_size)  8.72 us
  transfers between devices with their start and end apart: 2, of which 1 were waited for; matrix products, arithmetic and copies ran while one was open for 20% of the time, Pallas kernels for 0%

profile of v1, /device:TPU:0, one launch (start us, length us, event | category | flops | bytes accessed | tf_op | source)
XLA Modules:
  0.0 350.8 jit_solution(10480637136870091055)
XLA Ops:
  6.5 0.0 all-gather.2.cloned.1.call-start
  6.5 0.7 all-gather.2.cloned.1.call-update
  7.3 5.1 %stack.2 = bf16[128,16,2048]{2,1,0:T(8,128)(2,1)} broadcast(bf16[16,2048]{1,0:T(8,128)(2,1)} %param.7), dimensions={1,2} | broadcast | bytes 8454144 | tf_op jit(solution)/shard_map/stack | solution.py:23
  12.4 0.0 copy-start
  12.4 0.0 copy-start.1
  12.4 11.7 %all-to-all-start = ((bf16[128,16,2048]{2,1,0:T(8,128)(2,1)}), bf16[128,16,2048]{2,1,0:T(8,128)(2,1)}, u32[]{:S(2)}, u32[]{:S(2)}) async-start(bf16[128,16,2048]{2,1,0:T(8,128)(2,1)} %stack.2), calls=%async_computation | async-start | bytes 16777216 | tf_op jit(solution)/shard_map/all_to_all | solution.py:22
  24.1 0.0 copy-done
  24.1 0.1 copy.10
  24.2 0.1 compare_select_fusion
  24.2 0.1 copy.12
  24.3 0.1 reshape.46
  24.4 0.1 copy.11
  24.5 0.1 reshape.38
  24.6 0.0 copy-done.1
  24.6 0.1 fusion.7
  24.7 0.6 gather_fusion.1
  25.3 0.6 gather_fusion
  25.9 0.1 eq.15
  26.0 5.2 %multiply_multiply_fusion.1 = bf16[16,2,4,128,128]{4,3,2,1,0:T(8,128)(2,1)} fusion(bf16[16,2,4,128,128]{4,3,2,1,0:T(8,128)(2,1)} %param.6, bf16[2,4,128]{2,1,0:T(4,128)(2,1)S(1)} %bitcast.56, bf16[2,128]{1,0:T(2,128)(2,1)S(1)} %constant_dynamic-slice_fusion.1), kind=kLoop, calls=%fused_computation.14 | loop fusion | flops 4194304 | bytes 8391168 | tf_op jit(solution)/shard_map/mul | solution.py:40
  31.3 174.5 %all-to-all-done = bf16[128,16,2048]{2,1,0:T(8,128)(2,1)} async-done(((bf16[128,16,2048]{2,1,0:T(8,128)(2,1)}), bf16[128,16,2048]{2,1,0:T(8,128)(2,1)}, u32[]{:S(2)}, u32[]{:S(2)}) %all-to-all-start) | async-done | bytes 8388640 | tf_op jit(solution)/shard_map/all_to_all | solution.py:22
  205.7 6.6 %gather_fusion.2 = bf16[8,128,2048]{2,1,0:T(8,128)(2,1)} fusion(bf16[16,128,2048]{2,1,0:T(8,128)(2,1)} %bitcast.11, s32[1024]{0:T(1024)S(1)} %pad_clamp_fusion), kind=kCustom, calls=%fused_computation.2 | custom fusion | bytes 8388640 | tf_op jit(solution)/shard_map/gather | solution.py:44
  212.3 35.3 %while.10 = (s32[]{:T(128)}, bf16[2,8,2,128,2048]{4,3,2,1,0:T(8,128)(2,1)}, bf16[2,8,2,4,128,128]{5,4,3,2,1,0:T(8,128)(2,1)}, bf16[2,4,128,2048]{3,2,1,0:T(8,128)(2,1)}, s32[]{:T(128)}) while((s32[]{:T(128)}, bf16[2,8,2,128,2048]{4,3,2,1,0:T(8,128)(2,1)}, bf16[2,8,2,4,128,128]{5,4,3,2,1,0:T(8,128)(2,1)}, bf16[2,4,128,2048]{3,2,1,0:T(8,128)(2,1)}, ...), condition=%wide.region_1.2_spmd, body=%wide.region_0.1_spmd.sunk | while | flops 4299161600 | bytes 31458364 | solution.py:54
  212.3 9.2 %fusion.13 = bf16[1,8,2,128,2048]{4,3,1,2,0:T(8,128)(2,1)} fusion(bf16[2,4,128,2048]{3,2,1,0:T(8,128)(2,1)} %get-tuple-element.78, bf16[2,8,2,4,128,128]{5,4,3,2,1,0:T(8,128)(2,1)} %get-tuple-element.77, s32[]{:T(128)} %get-tuple-element.70), kind=kOutput, calls=%fused_computation.4.clone.1 | convolution fusion | flops 4299161600 | bytes 14680576 | tf_op jit(solution)/shard_map/while/body/eval_jaxpr/pmjab,mjbs->pmas/dot_general | solution.py:49
  221.6 8.2 %copy_dynamic-update-slice_fusion.2 = bf16[2,8,2,128,2048]{4,3,2,1,0:T(8,128)(2,1)} fusion(bf16[2,8,2,128,2048]{4,3,2,1,0:T(8,128)(2,1)} %get-tuple-element.71, s32[]{:T(128)} %get-tuple-element.70, bf16[1,8,2,128,2048]{4,3,1,2,0:T(8,128)(2,1)} %fusion.13), kind=kLoop, calls=%fused_computation.5.clone.1 | loop fusion | bytes 16777728 | tf_op jit(solution)/shard_map/while/body/jit(dynamic_update_index_in_dim)/dynamic_update_slice | solution.py:54
  229.8 9.2 %fusion.13 = bf16[1,8,2,128,2048]{4,3,1,2,0:T(8,128)(2,1)} fusion(bf16[2,4,128,2048]{3,2,1,0:T(8,128)(2,1)} %get-tuple-element.78, bf16[2,8,2,4,128,128]{5,4,3,2,1,0:T(8,128)(2,1)} %get-tuple-element.77, s32[]{:T(128)} %get-tuple-element.70), kind=kOutput, calls=%fused_computation.4.clone.1 | convolution fusion | flops 4299161600 | bytes 14680576 | tf_op jit(solution)/shard_map/while/body/eval_jaxpr/pmjab,mjbs->pmas/dot_general | solution.py:49
  239.1 8.6 %copy_dynamic-update-slice_fusion.2 = bf16[2,8,2,128,2048]{4,3,2,1,0:T(8,128)(2,1)} fusion(bf16[2,8,2,128,2048]{4,3,2,1,0:T(8,128)(2,1)} %get-tuple-element.71, s32[]{:T(128)} %get-tuple-element.70, bf16[1,8,2,128,2048]{4,3,1,2,0:T(8,128)(2,1)} %fusion.13), kind=kLoop, calls=%fused_computation.5.clone.1 | loop fusion | bytes 16777728 | tf_op jit(solution)/shard_map/while/body/jit(dynamic_update_index_in_dim)/dynamic_update_slice | solution.py:54
  247.7 9.6 %copy.29 = bf16[512,8,16,128]{3,2,1,0:T(8,128)(2,1)S(1)} copy(bf16[512,8,16,128]{3,1,2,0:T(8,128)(2,1)} %bitcast.52) | data formatting | bytes 33554432
  257.3 7.4 %bitcast_bitcast_fusion = bf16[16,256,16,128,1]{3,2,1,0,4:T(8,128)(2,1)} fusion(bf16[16,256,16,128]{3,2,1,0:T(8,128)(2,1)S(1)} %bitcast.50), kind=kLoop, calls=%fused_computation.12 | loop fusion | bytes 33554432 | tf_op jit(solution)/shard_map/reshape;reshape | solution.py:55
  264.8 0.0 all-gather.2.cloned.1.call-done
  264.8 24.2 %fusion.2 = f32[16,4,128,256,1]{3,2,0,1,4:T(8,128)} fusion(bf16[16,256,16,128,1]{3,2,1,0,4:T(8,128)(2,1)} %bitcast_bitcast_fusion, bf16[16,16,4,128,128]{4,3,2,1,0:T(8,128)(2,1)} %all-gather.2.cloned.1.call-done, bf16[16,4,128]{2,1,0:T(4,128)(2,1)S(1)} %bitcast.55, bf16[16,128]{1,0:T(8,128)(2,1)S(1)} %fusion.7), kind=kOutput, calls=%fused_computation.9 | convolution fusion | flops 8623489024 | bytes 58740736 | tf_op jit(solution)/shard_map/pmbc,pbjcn->mbjn/dot_general | solution.py:59
  288.9 7.6 %copy.22 = f32[16,4,128,256,1]{3,2,1,0,4:T(8,128)} copy(f32[16,4,128,256,1]{3,2,0,1,4:T(8,128)} %fusion.2) | data formatting | bytes 16777216 | tf_op jit(solution)/shard_map/pmbc,pbjcn->mbjn/dot_general | solution.py:59
  296.6 8.7 %copy.17 = f32[256,64,128]{2,1,0:T(8,128)} copy(f32[256,64,128]{0,2,1:T(8,128)} %bitcast.51) | data formatting | bytes 16777216 | tf_op jit(solution)/shard_map/reshape | solution.py:67
  305.3 5.1 %convolution_bitcast_fusion = f32[256,16,128]{2,1,0:T(8,128)S(1)} fusion(f32[256,64,128]{2,1,0:T(8,128)} %copy.17, s32[64]{0:T(128)S(1)} %eq.15), kind=kOutput, calls=%fused_computation.15 | convolution fusion | flops 402654208 | bytes 10486016 | tf_op jit(solution)/shard_map/mqn,qk->mkn/dot_general | solution.py:65
  310.4 1.5 reshape_reshape.11
  311.9 31.3 %all_to_all.10 = f32[16,16,2048]{2,1,0:T(8,128)S(1)} all-to-all(f32[16,16,2048]{2,1,0:T(8,128)} %reshape_reshape.11), channel_id=1, replica_groups=mesh['atom'=8,'aux'=16] {'aux'}, dimensions={0} | all-to-all | bytes 4194304 | tf_op jit(solution)/shard_map/all_to_all | solution.py:16
  343.2 0.8 reduce_sum.9
  (5 shorter events, 0.0 us)
Async XLA Ops:
  6.5 258.2 %all-gather.2.cloned.1.call-start = ((), (), s32[]{:S(2)}) async-start(), calls=%async_computation.2 | async-start | bytes 37748736 | tf_op jit(solution)/shard_map/all_gather | solution.py:56
  12.4 11.7 %copy-start = (s32[16,4]{0,1:T(4,128)S(1)}, s32[16,4]{0,1:T(4,128)}, u32[]{:S(2)}) copy-start(s32[16,4]{0,1:T(4,128)} %param.8) | copy-start | bytes 772
  12.4 12.2 %copy-start.1 = (s32[16]{0:T(128)S(1)}, s32[16]{0:T(128)}, u32[]{:S(2)}) copy-start(s32[16]{0:T(128)} %param.9) | copy-start | bytes 196
  12.4 193.4 %all-to-all-start = ((bf16[128,16,2048]{2,1,0:T(8,128)(2,1)}), bf16[128,16,2048]{2,1,0:T(8,128)(2,1)}, u32[]{:S(2)}, u32[]{:S(2)}) async-start(bf16[128,16,2048]{2,1,0:T(8,128)(2,1)} %stack.2), calls=%async_computation | async-start | bytes 16777216 | tf_op jit(solution)/shard_map/all_to_all | solution.py:22
Sparse Core Ops, SparseCore 0:
  9.0 244.5 all-gather.1
